TPU v7x, 32 devices: a whole 2x2x4 slice. The times are simulated.
32 devices in a mesh: dp: 4 (over z), fsdp: 8 (over y, x, core).
Axes of the slice: x: 2, y: 2, z: 4, core: 2. Of those that a mesh axis runs over, the one named last changes fastest.
Arguments:
- tokens: bfloat16 [8192, 768], P(('dp', 'fsdp')), may hold values from -6 to 6
- cotangent: bfloat16 [8192, 768], P(('dp', 'fsdp')), may hold values from -6 to 6
- routes: int32 [64, 2], P(('dp', 'fsdp')), may hold values from 0 to 15, as said below
- lengths: int32 [64, 3], P(('dp', 'fsdp')), may hold values from 1 to 64, 128 in all within a row
- buckets: int32 [255], replicated, may hold values from 0 to 511
- w_query: bfloat16 [768, 768], P(('dp', 'fsdp')), may hold values from -0.21875 to 0.21875
- w_key: bfloat16 [768, 768], P(('dp', 'fsdp')), may hold values from -0.21875 to 0.21875
- w_value: bfloat16 [768, 768], P(('dp', 'fsdp')), may hold values from -0.21875 to 0.21875
- w_output: bfloat16 [768, 768], P(('dp', 'fsdp')), may hold values from -1.25 to 1.25
- w_inner: bfloat16 [768, 3072], P(('dp', 'fsdp')), may hold values from -0.21875 to 0.21875
- w_outer: bfloat16 [3072, 768], P(('dp', 'fsdp')), may hold values from -0.109375 to 0.109375
- relative: bfloat16 [512, 768], P(('dp', 'fsdp')), may hold values from -6 to 6
- b_query: bfloat16 [768], P(('dp', 'fsdp')), may hold values from -0.59765625 to 0.59765625
- b_key: bfloat16 [768], P(('dp', 'fsdp')), may hold values from -0.59765625 to 0.59765625
- b_value: bfloat16 [768], P(('dp', 'fsdp')), may hold values from -0.59765625 to 0.59765625
- b_output: bfloat16 [768], P(('dp', 'fsdp')), may hold values from -0.59765625 to 0.59765625
- b_inner: bfloat16 [3072], P(('dp', 'fsdp')), may hold values from -0.59765625 to 0.59765625
- b_outer: bfloat16 [768], P(('dp', 'fsdp')), may hold values from -0.59765625 to 0.59765625
- attn_gain: bfloat16 [768], P(('dp', 'fsdp')), may hold values from 0.5 to 1.5
- attn_shift: bfloat16 [768], P(('dp', 'fsdp')), may hold values from -0.59765625 to 0.59765625
- ffn_gain: bfloat16 [768], P(('dp', 'fsdp')), may hold values from 0.5 to 1.5
- ffn_shift: bfloat16 [768], P(('dp', 'fsdp')), may hold values from -0.59765625 to 0.59765625
- rel_gain: bfloat16 [768], P(('dp', 'fsdp')), may hold values from 0.5 to 1.5
- rel_shift: bfloat16 [768], P(('dp', 'fsdp')), may hold values from -0.59765625 to 0.59765625
Outputs:
- output: bfloat16 [8192, 768], P(('dp', 'fsdp'))
- grad_input: bfloat16 [8192, 768], P(('dp', 'fsdp'))
- grad_w_query: float32 [768, 768], P(('dp', 'fsdp'))
- grad_w_key: float32 [768, 768], P(('dp', 'fsdp'))
- grad_w_value: float32 [768, 768], P(('dp', 'fsdp'))
- grad_w_output: float32 [768, 768], P(('dp', 'fsdp'))
- grad_w_inner: float32 [768, 3072], P(('dp', 'fsdp'))
- grad_w_outer: float32 [3072, 768], P(('dp', 'fsdp'))
- grad_relative: float32 [512, 768], P(('dp', 'fsdp'))
- grad_b_query: float32 [768], P(('dp', 'fsdp'))
- grad_b_key: float32 [768], P(('dp', 'fsdp'))
- grad_b_value: float32 [768], P(('dp', 'fsdp'))
- grad_b_output: float32 [768], P(('dp', 'fsdp'))
- grad_b_inner: float32 [3072], P(('dp', 'fsdp'))
- grad_b_outer: float32 [768], P(('dp', 'fsdp'))
- grad_attn_gain: float32 [768], P(('dp', 'fsdp'))
- grad_attn_shift: float32 [768], P(('dp', 'fsdp'))
- grad_ffn_gain: float32 [768], P(('dp', 'fsdp'))
- grad_ffn_shift: float32 [768], P(('dp', 'fsdp'))
- grad_rel_gain: float32 [768], P(('dp', 'fsdp'))
- grad_rel_shift: float32 [768], P(('dp', 'fsdp'))
Inputs may be any that keep to these rules, and one draw needn't show every extreme that they name: `routes`: entry k of a row gives t * 2 + p: page k of that device's micro-batch goes to slot p of the bin of fsdp index t in the same dp group and micro-batch. Within a dp group and micro-batch every value occurs once, and a device sends at most one page of a micro-batch to any device. Each row is the lengths of the 3 sequences of one bin, in order, summing to 128. `buckets`: entry 127 + d is the bucket of the distance d.
All inputs are finite; a program needn't handle non-finite values.
Results may differ from a plain program's by a relative error of at most 0.02.
Values may be sent and summed in bfloat16 or wider, within the bound.
No kernel may reach another device: no remote copies, remote signals or barrier semaphores. Data moves between devices by JAX's collectives and lax.ppermute only.
A program may use at most 192 MiB of HBM per device.

v0:
```python
import jax
import jax.numpy as jnp
from jax import lax
from jax.sharding import PartitionSpec as P

HEADS = 12
HEAD = 64
POS = 256
MICRO = 2
PAGE = 64


EPS = 1e-07
ROOT_HALF = 0.7071067811865476
ROOT_TWO_PI = 2.5066282746310002


def product(left, right):
    return jnp.dot(left, right, preferred_element_type=jnp.float32)


def left_sum(left, right):
    return lax.dot_general(
        left, right, (((0,), (0,)), ((), ())), preferred_element_type=jnp.float32
    )


def right_sum(left, right):
    return lax.dot_general(
        left, right, (((1,), (1,)), ((), ())), preferred_element_type=jnp.float32
    )


def column_sum(value):
    return jnp.sum(value.astype(jnp.float32), axis=0)


def normalize_keep(value, gain, shift):
    average = jnp.mean(value, axis=-1, keepdims=True)
    centered = value - average
    inv_dev = lax.rsqrt(jnp.mean(centered * centered, axis=-1, keepdims=True) + EPS)
    unit_row = centered * inv_dev
    return (unit_row * gain + shift, unit_row, inv_dev)


def normalize_back(grad_out, unit_row, inv_dev, gain):
    scaled = grad_out * gain
    mixed = scaled - jnp.mean(scaled, axis=-1, keepdims=True)
    mixed = mixed - unit_row * jnp.mean(scaled * unit_row, axis=-1, keepdims=True)
    return (mixed * inv_dev, jnp.sum(grad_out * unit_row, axis=0), jnp.sum(grad_out, axis=0))


def gelu_exact(value):
    return 0.5 * value * (1.0 + lax.erf(value * ROOT_HALF))


def gelu_slope(value):
    return (
        0.5 * (1.0 + lax.erf(value * ROOT_HALF))
        + value * jnp.exp(-0.5 * value * value) / ROOT_TWO_PI
    )


def same_layout(rows_bin, seq_lens):
    position = jnp.arange(rows_bin, dtype=jnp.int32)
    boundary = jnp.cumsum(seq_lens)[:-1]
    segment = jnp.sum((position[:, None] >= boundary[None, :]).astype(jnp.int32), axis=1)
    return segment[:, None] == segment[None, :]


def skew_rows(dist):
    heads, rows, span = dist.shape
    flipped = jnp.flip(dist, axis=-1).reshape(heads, rows * span)
    cut = flipped[:, rows - 1 : rows - 1 + rows * (span - 1)].reshape(heads, rows, span - 1)
    return cut[:, :, :rows]


def straighten_relative_rows(square):
    heads, rows, _ = square.shape
    span = 2 * rows - 1
    wide = jnp.pad(square, ((0, 0), (0, 0), (0, span - 1 - rows))).reshape(heads, rows * (span - 1))
    full = jnp.pad(wide, ((0, 0), (rows - 1, 1))).reshape(heads, rows, span)
    return jnp.flip(full, axis=-1)


def score_all(query_rows, keyed, pos_query, position_key, buckets):
    score_scale = (3.0 * HEAD) ** (-0.5)
    content = jnp.einsum("ihd,jhd->hij", query_rows, keyed, preferred_element_type=jnp.float32)
    content_position_score = jnp.einsum(
        "tsk,nsk->stn", query_rows, position_key, preferred_element_type=jnp.float32
    )
    pos_cont = jnp.einsum("jhd,bhd->hjb", keyed, pos_query, preferred_element_type=jnp.float32)
    to_pos = skew_rows(jnp.take(content_position_score, buckets, axis=2))
    to_cont = skew_rows(jnp.take(pos_cont, buckets, axis=2))
    return score_scale * (content + to_pos + jnp.swapaxes(to_cont, 1, 2))


def layer_forward(full, inputs, seq_lens, buckets):
    (
        w_query,
        w_key,
        w_value,
        w_output,
        w_inner,
        w_outer,
        relative,
        b_query,
        b_key,
        b_value,
        b_output,
        b_inner,
        b_outer,
        attn_gain,
        attn_shift,
        ffn_gain,
        ffn_shift,
        rel_gain,
        rel_shift,
    ) = full
    rows_bin = inputs.shape[0]
    width = inputs.shape[1]
    rel_out, rel_unit, rel_inv = normalize_keep(
        relative.astype(jnp.float32), rel_gain.astype(jnp.float32), rel_shift.astype(jnp.float32)
    )
    rel_low = rel_out.astype(jnp.bfloat16)
    query_rows = (
        (product(inputs, w_query) + b_query.astype(jnp.float32))
        .astype(jnp.bfloat16)
        .reshape(rows_bin, HEADS, HEAD)
    )
    keyed = (
        (product(inputs, w_key) + b_key.astype(jnp.float32))
        .astype(jnp.bfloat16)
        .reshape(rows_bin, HEADS, HEAD)
    )
    valued = (
        (product(inputs, w_value) + b_value.astype(jnp.float32))
        .astype(jnp.bfloat16)
        .reshape(rows_bin, HEADS, HEAD)
    )
    pos_query = (
        (product(rel_low, w_query) + b_query.astype(jnp.float32))
        .astype(jnp.bfloat16)
        .reshape(2 * POS, HEADS, HEAD)
    )
    position_key = (
        (product(rel_low, w_key) + b_key.astype(jnp.float32))
        .astype(jnp.bfloat16)
        .reshape(2 * POS, HEADS, HEAD)
    )
    same_seq = same_layout(rows_bin, seq_lens)
    scores = score_all(query_rows, keyed, pos_query, position_key, buckets)
    masked = jnp.where(same_seq[None], scores, -1e30)
    row_max = jnp.max(masked, axis=-1, keepdims=True)
    log_total = row_max + jnp.log(jnp.sum(jnp.exp(masked - row_max), axis=-1, keepdims=True))
    attn_prob = jnp.exp(masked - log_total)
    context = jnp.einsum(
        "hij,jhd->ihd", attn_prob.astype(jnp.bfloat16), valued, preferred_element_type=jnp.float32
    )
    context = context.reshape(rows_bin, width).astype(jnp.bfloat16)
    attended = product(context, w_output) + b_output.astype(jnp.float32)
    hidden, unit_one, inv_one = normalize_keep(
        attended + inputs.astype(jnp.float32),
        attn_gain.astype(jnp.float32),
        attn_shift.astype(jnp.float32),
    )
    hidden_low = hidden.astype(jnp.bfloat16)
    inner_pre = product(hidden_low, w_inner) + b_inner.astype(jnp.float32)
    active = gelu_exact(inner_pre).astype(jnp.bfloat16)
    outer_out = product(active, w_outer) + b_outer.astype(jnp.float32)
    result, unit_two, inv_two = normalize_keep(
        outer_out + hidden, ffn_gain.astype(jnp.float32), ffn_shift.astype(jnp.float32)
    )
    saved = (
        inputs,
        rel_low,
        rel_unit,
        rel_inv,
        query_rows,
        keyed,
        valued,
        pos_query,
        position_key,
        same_seq,
        log_total,
        context,
        unit_one,
        inv_one,
        hidden_low,
        inner_pre,
        active,
        unit_two,
        inv_two,
    )
    return (result, saved)


def layer_backward(full, saved, grad_out, buckets):
    (
        w_query,
        w_key,
        w_value,
        w_output,
        w_inner,
        w_outer,
        relative,
        b_query,
        b_key,
        b_value,
        b_output,
        b_inner,
        b_outer,
        attn_gain,
        attn_shift,
        ffn_gain,
        ffn_shift,
        rel_gain,
        rel_shift,
    ) = full
    (
        inputs,
        rel_low,
        rel_unit,
        rel_inv,
        query_rows,
        keyed,
        valued,
        pos_query,
        position_key,
        same_seq,
        log_total,
        context,
        unit_one,
        inv_one,
        hidden_low,
        inner_pre,
        active,
        unit_two,
        inv_two,
    ) = saved
    rows_bin = inputs.shape[0]
    width = inputs.shape[1]
    score_scale = (3.0 * HEAD) ** (-0.5)
    grad_res2, grad_ffn_gain, grad_ffn_shift = normalize_back(
        grad_out, unit_two, inv_two, ffn_gain.astype(jnp.float32)
    )
    grad_outer = grad_res2.astype(jnp.bfloat16)
    grad_w_outer = left_sum(active, grad_outer)
    grad_b_outer = column_sum(grad_outer)
    grad_inner = (right_sum(grad_outer, w_outer) * gelu_slope(inner_pre)).astype(jnp.bfloat16)
    grad_w_inner = left_sum(hidden_low, grad_inner)
    grad_b_inner = column_sum(grad_inner)
    grad_hidden = right_sum(grad_inner, w_inner) + grad_res2
    grad_res1, grad_attn_gain, grad_attn_shift = normalize_back(
        grad_hidden, unit_one, inv_one, attn_gain.astype(jnp.float32)
    )
    grad_att = grad_res1.astype(jnp.bfloat16)
    grad_w_output = left_sum(context, grad_att)
    grad_b_output = column_sum(grad_att)
    grad_context = right_sum(grad_att, w_output).astype(jnp.bfloat16).reshape(rows_bin, HEADS, HEAD)
    scores = score_all(query_rows, keyed, pos_query, position_key, buckets)
    masked = jnp.where(same_seq[None], scores, -1e30)
    attn_prob = jnp.exp(masked - log_total)
    grad_prob = jnp.einsum("ihd,jhd->hij", grad_context, valued, preferred_element_type=jnp.float32)
    grad_value = jnp.einsum(
        "hij,ihd->jhd",
        attn_prob.astype(jnp.bfloat16),
        grad_context,
        preferred_element_type=jnp.float32,
    ).astype(jnp.bfloat16)
    row_dot = jnp.sum(attn_prob * grad_prob, axis=-1, keepdims=True)
    score_gradient = (attn_prob * (grad_prob - row_dot)).astype(jnp.bfloat16)
    indicator_matrix = (buckets[:, None] == jnp.arange(2 * POS, dtype=jnp.int32)[None, :]).astype(
        jnp.bfloat16
    )
    content_position_gradient = (
        score_scale
        * jnp.einsum(
            "mgu,uw->mgw",
            straighten_relative_rows(score_gradient),
            indicator_matrix,
            preferred_element_type=jnp.float32,
        )
    ).astype(jnp.bfloat16)
    grad_pos_cont = (
        score_scale
        * jnp.einsum(
            "hjk,kb->hjb",
            straighten_relative_rows(jnp.swapaxes(score_gradient, 1, 2)),
            indicator_matrix,
            preferred_element_type=jnp.float32,
        )
    ).astype(jnp.bfloat16)
    grad_query = score_scale * jnp.einsum(
        "hij,jhd->ihd", score_gradient, keyed, preferred_element_type=jnp.float32
    )
    grad_query = grad_query + jnp.einsum(
        "pqg,gpl->qpl", content_position_gradient, position_key, preferred_element_type=jnp.float32
    )
    grad_key = score_scale * jnp.einsum(
        "hij,ihd->jhd", score_gradient, query_rows, preferred_element_type=jnp.float32
    )
    grad_key = grad_key + jnp.einsum(
        "hjb,bhd->jhd", grad_pos_cont, pos_query, preferred_element_type=jnp.float32
    )
    grad_pos_key = jnp.einsum(
        "len,elm->nlm", content_position_gradient, query_rows, preferred_element_type=jnp.float32
    )
    grad_pos_query = jnp.einsum(
        "hjb,jhd->bhd", grad_pos_cont, keyed, preferred_element_type=jnp.float32
    )
    grad_query = grad_query.astype(jnp.bfloat16).reshape(rows_bin, width)
    grad_key = grad_key.astype(jnp.bfloat16).reshape(rows_bin, width)
    grad_value = grad_value.reshape(rows_bin, width)
    grad_pos_key = grad_pos_key.astype(jnp.bfloat16).reshape(2 * POS, width)
    grad_pos_query = grad_pos_query.astype(jnp.bfloat16).reshape(2 * POS, width)
    grad_w_query = left_sum(inputs, grad_query) + left_sum(rel_low, grad_pos_query)
    grad_b_query = column_sum(grad_query) + column_sum(grad_pos_query)
    grad_w_key = left_sum(inputs, grad_key) + left_sum(rel_low, grad_pos_key)
    grad_b_key = column_sum(grad_key) + column_sum(grad_pos_key)
    grad_w_value = left_sum(inputs, grad_value)
    grad_b_value = column_sum(grad_value)
    grad_in = (
        grad_res1
        + right_sum(grad_query, w_query)
        + right_sum(grad_key, w_key)
        + right_sum(grad_value, w_value)
    )
    grad_rel_low = right_sum(grad_pos_query, w_query) + right_sum(grad_pos_key, w_key)
    grad_relative, grad_rel_gain, grad_rel_shift = normalize_back(
        grad_rel_low, rel_unit, rel_inv, rel_gain.astype(jnp.float32)
    )
    grads = (
        grad_w_query,
        grad_w_key,
        grad_w_value,
        grad_w_output,
        grad_w_inner,
        grad_w_outer,
        grad_relative,
        grad_b_query,
        grad_b_key,
        grad_b_value,
        grad_b_output,
        grad_b_inner,
        grad_b_outer,
        grad_attn_gain,
        grad_attn_shift,
        grad_ffn_gain,
        grad_ffn_shift,
        grad_rel_gain,
        grad_rel_shift,
    )
    return (grad_in, grads)


def dispatch_plan(route_row, groups, pages):
    target = route_row // pages
    slot_pos = route_row % pages
    chosen = target[None, :] == jnp.arange(groups, dtype=jnp.int32)[:, None]
    sent_slot = jnp.sum(jnp.where(chosen, slot_pos[None, :] + 1, 0), axis=1).astype(jnp.bfloat16)
    return (chosen.astype(jnp.bfloat16), sent_slot)


def on_device(
    tokens,
    cotangent,
    routes,
    lengths,
    buckets,
    w_query,
    w_key,
    w_value,
    w_output,
    w_inner,
    w_outer,
    relative,
    b_query,
    b_key,
    b_value,
    b_output,
    b_inner,
    b_outer,
    attn_gain,
    attn_shift,
    ffn_gain,
    ffn_shift,
    rel_gain,
    rel_shift,
):
    shards = (
        w_query,
        w_key,
        w_value,
        w_output,
        w_inner,
        w_outer,
        relative,
        b_query,
        b_key,
        b_value,
        b_output,
        b_inner,
        b_outer,
        attn_gain,
        attn_shift,
        ffn_gain,
        ffn_shift,
        rel_gain,
        rel_shift,
    )
    groups = lax.axis_size("fsdp")
    rows_bin = tokens.shape[0] // MICRO
    pages = rows_bin // PAGE
    width = tokens.shape[1]
    totals = None
    outputs = []
    grads_back = []
    for micro_idx in range(MICRO):
        own_rows = tokens[micro_idx * rows_bin : (micro_idx + 1) * rows_bin].reshape(
            pages, PAGE, width
        )
        own_grads = cotangent[micro_idx * rows_bin : (micro_idx + 1) * rows_bin].reshape(
            pages, PAGE, width
        )
        pick, sent_slot = dispatch_plan(routes[micro_idx], groups, pages)
        send_rows = jnp.einsum(
            "gk,krd->grd", pick, own_rows, preferred_element_type=jnp.float32
        ).astype(jnp.bfloat16)
        send_grads = jnp.einsum(
            "gk,krd->grd", pick, own_grads, preferred_element_type=jnp.float32
        ).astype(jnp.bfloat16)
        got_rows, got_grads, got_slot = (
            lax.all_to_all(send_rows, "fsdp", split_axis=0, concat_axis=0, tiled=True),
            lax.all_to_all(send_grads, "fsdp", split_axis=0, concat_axis=0, tiled=True),
            lax.all_to_all(sent_slot, "fsdp", split_axis=0, concat_axis=0, tiled=True),
        )
        slot_ids = (jnp.arange(pages, dtype=jnp.int32) + 1).astype(jnp.float32)
        place = (got_slot.astype(jnp.float32)[None, :] == slot_ids[:, None]).astype(jnp.bfloat16)
        bin_rows = jnp.einsum("ps,srd->prd", place, got_rows, preferred_element_type=jnp.float32)
        bin_rows = bin_rows.reshape(rows_bin, width).astype(jnp.bfloat16)
        bin_grads = jnp.einsum("ps,srd->prd", place, got_grads, preferred_element_type=jnp.float32)
        bin_grads = bin_grads.reshape(rows_bin, width)
        full = (
            lax.all_gather(shards[0], ("dp", "fsdp"), axis=0, tiled=True),
            lax.all_gather(shards[1], ("dp", "fsdp"), axis=0, tiled=True),
            lax.all_gather(shards[2], ("dp", "fsdp"), axis=0, tiled=True),
            lax.all_gather(shards[3], ("dp", "fsdp"), axis=0, tiled=True),
            lax.all_gather(shards[4], ("dp", "fsdp"), axis=0, tiled=True),
            lax.all_gather(shards[5], ("dp", "fsdp"), axis=0, tiled=True),
            lax.all_gather(shards[6], ("dp", "fsdp"), axis=0, tiled=True),
            lax.all_gather(shards[7], ("dp", "fsdp"), axis=0, tiled=True),
            lax.all_gather(shards[8], ("dp", "fsdp"), axis=0, tiled=True),
            lax.all_gather(shards[9], ("dp", "fsdp"), axis=0, tiled=True),
            lax.all_gather(shards[10], ("dp", "fsdp"), axis=0, tiled=True),
            lax.all_gather(shards[11], ("dp", "fsdp"), axis=0, tiled=True),
            lax.all_gather(shards[12], ("dp", "fsdp"), axis=0, tiled=True),
            lax.all_gather(shards[13], ("dp", "fsdp"), axis=0, tiled=True),
            lax.all_gather(shards[14], ("dp", "fsdp"), axis=0, tiled=True),
            lax.all_gather(shards[15], ("dp", "fsdp"), axis=0, tiled=True),
            lax.all_gather(shards[16], ("dp", "fsdp"), axis=0, tiled=True),
            lax.all_gather(shards[17], ("dp", "fsdp"), axis=0, tiled=True),
            lax.all_gather(shards[18], ("dp", "fsdp"), axis=0, tiled=True),
        )
        result, saved = layer_forward(full, bin_rows, lengths[micro_idx], buckets)
        again = (
            lax.all_gather(shards[0], ("dp", "fsdp"), axis=0, tiled=True),
            lax.all_gather(shards[1], ("dp", "fsdp"), axis=0, tiled=True),
            lax.all_gather(shards[2], ("dp", "fsdp"), axis=0, tiled=True),
            lax.all_gather(shards[3], ("dp", "fsdp"), axis=0, tiled=True),
            lax.all_gather(shards[4], ("dp", "fsdp"), axis=0, tiled=True),
            lax.all_gather(shards[5], ("dp", "fsdp"), axis=0, tiled=True),
            lax.all_gather(shards[6], ("dp", "fsdp"), axis=0, tiled=True),
            lax.all_gather(shards[7], ("dp", "fsdp"), axis=0, tiled=True),
            lax.all_gather(shards[8], ("dp", "fsdp"), axis=0, tiled=True),
            lax.all_gather(shards[9], ("dp", "fsdp"), axis=0, tiled=True),
            lax.all_gather(shards[10], ("dp", "fsdp"), axis=0, tiled=True),
            lax.all_gather(shards[11], ("dp", "fsdp"), axis=0, tiled=True),
            lax.all_gather(shards[12], ("dp", "fsdp"), axis=0, tiled=True),
            lax.all_gather(shards[13], ("dp", "fsdp"), axis=0, tiled=True),
            lax.all_gather(shards[14], ("dp", "fsdp"), axis=0, tiled=True),
            lax.all_gather(shards[15], ("dp", "fsdp"), axis=0, tiled=True),
            lax.all_gather(shards[16], ("dp", "fsdp"), axis=0, tiled=True),
            lax.all_gather(shards[17], ("dp", "fsdp"), axis=0, tiled=True),
            lax.all_gather(shards[18], ("dp", "fsdp"), axis=0, tiled=True),
        )
        grad_in, grads = layer_backward(again, saved, bin_grads, buckets)
        if totals is None:
            totals = grads
        else:
            totals = jax.tree.map(jnp.add, totals, grads)
        result_pages = result.astype(jnp.bfloat16).reshape(pages, PAGE, width)
        grad_pages = grad_in.astype(jnp.bfloat16).reshape(pages, PAGE, width)
        ret_rows = jnp.einsum(
            "ps,prd->srd", place, result_pages, preferred_element_type=jnp.float32
        ).astype(jnp.bfloat16)
        ret_grads = jnp.einsum(
            "ps,prd->srd", place, grad_pages, preferred_element_type=jnp.float32
        ).astype(jnp.bfloat16)
        back_rows, back_grads = (
            lax.all_to_all(ret_rows, "fsdp", split_axis=0, concat_axis=0, tiled=True),
            lax.all_to_all(ret_grads, "fsdp", split_axis=0, concat_axis=0, tiled=True),
        )
        outputs.append(
            jnp.einsum("gk,grd->krd", pick, back_rows, preferred_element_type=jnp.float32)
            .reshape(rows_bin, width)
            .astype(jnp.bfloat16)
        )
        grads_back.append(
            jnp.einsum("gk,grd->krd", pick, back_grads, preferred_element_type=jnp.float32)
            .reshape(rows_bin, width)
            .astype(jnp.bfloat16)
        )
    summed = lax.psum_scatter(totals, ("dp", "fsdp"), scatter_dimension=0, tiled=True)
    return (jnp.concatenate(outputs, axis=0), jnp.concatenate(grads_back, axis=0)) + tuple(summed)


def solution(mesh):
    in_specs = (
        P(("dp", "fsdp"), None),
        P(("dp", "fsdp"), None),
        P(("dp", "fsdp"), None),
        P(("dp", "fsdp"), None),
        P(),
        P(("dp", "fsdp"), None),
        P(("dp", "fsdp"), None),
        P(("dp", "fsdp"), None),
        P(("dp", "fsdp"), None),
        P(("dp", "fsdp"), None),
        P(("dp", "fsdp"), None),
        P(("dp", "fsdp"), None),
        P(("dp", "fsdp")),
        P(("dp", "fsdp")),
        P(("dp", "fsdp")),
        P(("dp", "fsdp")),
        P(("dp", "fsdp")),
        P(("dp", "fsdp")),
        P(("dp", "fsdp")),
        P(("dp", "fsdp")),
        P(("dp", "fsdp")),
        P(("dp", "fsdp")),
        P(("dp", "fsdp")),
        P(("dp", "fsdp")),
    )
    out_specs = (
        P(("dp", "fsdp"), None),
        P(("dp", "fsdp"), None),
        P(("dp", "fsdp"), None),
        P(("dp", "fsdp"), None),
        P(("dp", "fsdp"), None),
        P(("dp", "fsdp"), None),
        P(("dp", "fsdp"), None),
        P(("dp", "fsdp"), None),
        P(("dp", "fsdp"), None),
        P(("dp", "fsdp")),
        P(("dp", "fsdp")),
        P(("dp", "fsdp")),
        P(("dp", "fsdp")),
        P(("dp", "fsdp")),
        P(("dp", "fsdp")),
        P(("dp", "fsdp")),
        P(("dp", "fsdp")),
        P(("dp", "fsdp")),
        P(("dp", "fsdp")),
        P(("dp", "fsdp")),
        P(("dp", "fsdp")),
    )
    return jax.shard_map(
        on_device, mesh=mesh, in_specs=in_specs, out_specs=out_specs, check_vma=False
    )
```

profile of v0, /device:TPU:0, one launch (start us, length us, event | category | flops | bytes accessed | tf_op | source)
XLA Modules:
  0.0 1349.8 jit_solution(1782000252893747233)
XLA Ops:
  13.5 5.2 all-to-all-start.3
  23.2 44.8 %all_gather.44 = bf16[512,768]{1,0:T(8,128)(2,1)S(1)} all-gather(bf16[16,768]{1,0:T(8,128)(2,1)S(1)} %copy-done.129), channel_id=1, replica_groups=mesh['dp'=4,'fsdp'=8] {'dp','fsdp'}, dimensions={0}, use_global_device_ids=true | all-gather | bytes 811008 | tf_op jit(solution)/shard_map/all_gather | solution.py:451
  68.4 7.0 all_to_all.52
  82.3 9.5 all-to-all-done.8
  97.1 11.8 all-to-all-done.6
  116.3 42.7 %all-reduce.33 = (bf16[768]{0:T(1024)(128)(2,1)S(1)}, bf16[768]{0:T(1024)(128)(2,1)S(1)}, bf16[768]{0:T(1024)(128)(2,1)S(1)}, bf16[768]{0:T(1024)(128)(2,1)S(1)}...) all-reduce(bf16[768]{0:T(1024)(128)(2,1)S(1)} %dynamic-update-slice, ...), channel_id=1, replica_groups=mesh['dp'=4,'fsdp'=8] {'dp','fsdp'}, use_global_device_ids=true, to_apply=%add.8 | all-reduce | flops 11520 | bytes 46080
  169.4 11.7 reduce-scatter.20.cloned.1.call-start
  196.7 5.2 copy.421
  210.8 5.1 copy.436
  227.2 5.1 copy.439
  240.7 5.1 copy.417
  250.0 6.0 select_bitcast_fusion.2
  267.2 5.1 reshape.516
  283.9 5.1 reshape.513
  301.0 5.3 reshape.526
  336.9 39.4 %all-gather.17.cloned.1.call-done = bf16[3072,768]{1,0:T(8,128)(2,1)} async-done(((bf16[96,768]{1,0:T(8,128)(2,1)}), bf16[3072,768]{1,0:T(8,128)(2,1)}) %all-gather.17.cloned.1.call-update) | async-done | bytes 4718608 | tf_op jit(solution)/shard_map/all_gather | solution.py:450
  420.1 12.9 reverse
  447.7 12.5 reverse.1
  483.2 12.6 reverse.2
  510.5 12.5 reverse.3
  577.5 5.2 convolution_add_fusion.1
  586.7 5.0 convolution_add_fusion
  604.2 7.8 all-to-all-done.5
  618.2 10.2 all-to-all-done.2
  634.2 42.8 %all-reduce.32 = (f32[768]{0:T(1024)S(1)}, f32[768]{0:T(1024)S(1)}, f32[768]{0:T(1024)S(1)}, f32[768]{0:T(1024)S(1)}, f32[3072]{0:T(1024)S(1)}, /*index=5*/f32[7...) all-reduce(f32[768]{0:T(1024)S(1)} %add.565, ...), channel_id=9, replica_groups=mesh['dp'=4,'fsdp'=8] {'dp','fsdp'}, use_global_device_ids=true, to_apply=%region_45.47.clone | all-reduce | flops 11520 | bytes 92160
  690.8 13.7 %all-to-all-done.7 = bf16[8,64,768]{2,1,0:T(8,128)(2,1)S(1)} async-done(((bf16[8,64,768]{2,1,0:T(8,128)(2,1)}), bf16[8,64,768]{2,1,0:T(8,128)(2,1)S(1)}, u32[]{:S(2)}, u32[]{:S(2)}) %all-to-all-start.7) | async-done | bytes 786464 | tf_op jit(solution)/shard_map/all_to_all | solution.py:502
  706.7 40.1 %reduce-scatter.8.cloned.1.call-done = f32[24,768]{1,0:T(8,128)} async-done(((f32[768,768]{1,0:T(8,128)}), f32[24,768]{1,0:T(8,128)}) %reduce-scatter.8.cloned.1.call-update) | async-done | bytes 73744 | tf_op jit(solution)/shard_map/reduce_scatter | solution.py:514
  746.8 104.8 %reduce-scatter.10.cloned.1.call-done = f32[24,768]{1,0:T(8,128)} async-done(((f32[768,768]{1,0:T(8,128)}), f32[24,768]{1,0:T(8,128)}) %reduce-scatter.10.cloned.1.call-update) | async-done | bytes 73744 | tf_op jit(solution)/shard_map/reduce_scatter | solution.py:514
  851.6 103.8 %reduce-scatter.12.cloned.1.call-done = f32[24,768]{1,0:T(8,128)} async-done(((f32[768,768]{1,0:T(8,128)}), f32[24,768]{1,0:T(8,128)}) %reduce-scatter.12.cloned.1.call-update) | async-done | bytes 73744 | tf_op jit(solution)/shard_map/reduce_scatter | solution.py:514
  955.4 104.8 %reduce-scatter.14.cloned.1.call-done = f32[24,768]{1,0:T(8,128)} async-done(((f32[768,768]{1,0:T(8,128)}), f32[24,768]{1,0:T(8,128)}) %reduce-scatter.14.cloned.1.call-update) | async-done | bytes 73744 | tf_op jit(solution)/shard_map/reduce_scatter | solution.py:514
  1060.2 140.7 %reduce-scatter.16.cloned.1.call-done = f32[24,3072]{1,0:T(8,128)} async-done(((f32[768,3072]{1,0:T(8,128)}), f32[24,3072]{1,0:T(8,128)}) %reduce-scatter.16.cloned.1.call-update) | async-done | bytes 294928 | tf_op jit(solution)/shard_map/reduce_scatter | solution.py:514
  1200.9 142.1 %reduce-scatter.18.cloned.1.call-done = f32[96,768]{1,0:T(8,128)} async-done(((f32[3072,768]{1,0:T(8,128)}), f32[96,768]{1,0:T(8,128)}) %reduce-scatter.18.cloned.1.call-update) | async-done | bytes 294928 | tf_op jit(solution)/shard_map/reduce_scatter | solution.py:514
  (729 shorter events, 347.3 us)
Async XLA Ops:
  7.2 180.4 %all-gather.7.cloned.1.call-start = ((), (), s32[]{:S(2)}) async-start(), calls=%async_computation.17 | async-start | bytes 1216512 | tf_op jit(solution)/shard_map/all_gather | solution.py:447
  7.9 182.2 %all-gather.11.cloned.1.call-start = ((), (), s32[]{:S(2)}) async-start(), calls=%async_computation.19 | async-start | bytes 1216512 | tf_op jit(solution)/shard_map/all_gather | solution.py:446
  8.7 183.2 %all-gather.9.cloned.1.call-start = ((), (), s32[]{:S(2)}) async-start(), calls=%async_computation.18 | async-start | bytes 1216512 | tf_op jit(solution)/shard_map/all_gather | solution.py:445
  9.4 315.2 %all-gather.13.cloned.1.call-start = ((), (), s32[]{:S(2)}) async-start(), calls=%async_computation.20 | async-start | bytes 1216512 | tf_op jit(solution)/shard_map/all_gather | solution.py:448
  10.0 322.6 %all-gather.15.cloned.1.call-start = ((), (), s32[]{:S(2)}) async-start(), calls=%async_computation.21 | async-start | bytes 4866048 | tf_op jit(solution)/shard_map/all_gather | solution.py:449
  12.7 83.8 %copy-start.165 = (s32[2]{0:T(128)}, s32[2]{0:T(128)S(1)}, u32[]{:S(2)}) copy-start(s32[2]{0:T(128)S(1)} %fusion.136) | copy-start | bytes 28
  13.5 54.9 %all-to-all-start.3 = ((bf16[8,1,1]{2,1,0:T(2,128)(2,1)}), bf16[8,1,1]{2,1,0:T(2,128)(2,1)S(1)}, u32[]{:S(2)}, u32[]{:S(2)}) async-start(bf16[8,1,1]{2,1,0:T(2,128)(2,1)} %copy.428), calls=%async_computation.3 | async-start | bytes 8192 | tf_op jit(solution)/shard_map/all_to_all | solution.py:436
  18.7 357.7 %all-gather.17.cloned.1.call-start = ((), (), s32[]{:S(2)}) async-start(), calls=%async_computation.22 | async-start | bytes 4866048 | tf_op jit(solution)/shard_map/all_gather | solution.py:450
  21.9 46.0 %copy-start.183 = (s32[255]{0:T(256)S(1)}, s32[255]{0:T(256)}, u32[]{:S(2)}) copy-start(s32[255]{0:T(256)} %param.30) | copy-start | bytes 3064
  21.9 46.0 %copy-start.182 = (s32[2,3]{1,0:T(2,128)S(1)}, s32[2,3]{1,0:T(2,128)}, u32[]{:S(2)}) copy-start(s32[2,3]{1,0:T(2,128)} %param.29) | copy-start | bytes 76
  67.9 124.0 %copy-start.24 = (bf16[512,768]{1,0:T(8,128)(2,1)}, bf16[512,768]{1,0:T(8,128)(2,1)S(1)}, u32[]{:S(2)}) copy-start(bf16[512,768]{1,0:T(8,128)(2,1)S(1)} %all_gather.44) | copy-start | bytes 2359300
  75.4 16.3 %all-to-all-start.8 = ((bf16[8,64,768]{2,1,0:T(8,128)(2,1)}), bf16[8,64,768]{2,1,0:T(8,128)(2,1)S(1)}, u32[]{:S(2)}, u32[]{:S(2)}) async-start(bf16[8,64,768]{2,1,0:T(8,128)(2,1)} %copy.461), calls=%async_computation.8 | async-start | bytes 1572864 | tf_op jit(solution)/shard_map/all_to_all | solution.py:435
  91.7 17.1 %all-to-all-start.6 = ((bf16[8,64,768]{2,1,0:T(8,128)(2,1)}), bf16[8,64,768]{2,1,0:T(8,128)(2,1)S(1)}, u32[]{:S(2)}, u32[]{:S(2)}) async-start(bf16[8,64,768]{2,1,0:T(8,128)(2,1)} %copy.447), calls=%async_computation.6 | async-start | bytes 1572864 | tf_op jit(solution)/shard_map/all_to_all | solution.py:435
  109.8 56.0 %all-to-all-start.1 = ((bf16[8,64,768]{2,1,0:T(8,128)(2,1)}), bf16[8,64,768]{2,1,0:T(8,128)(2,1)S(1)}, u32[]{:S(2)}, u32[]{:S(2)}) async-start(bf16[8,64,768]{2,1,0:T(8,128)(2,1)} %copy.410), calls=%async_computation.1 | async-start | bytes 1572864 | tf_op jit(solution)/shard_map/all_to_all | solution.py:434
  113.4 72.2 %copy-start.124 = (f32[2]{0:T(128)}, f32[2]{0:T(128)S(1)}, u32[]{:S(2)}) copy-start(f32[2]{0:T(128)S(1)} %add_convert_fusion.4) | copy-start | bytes 28
  165.8 19.7 %all-to-all-start.4 = ((bf16[8,64,768]{2,1,0:T(8,128)(2,1)}), bf16[8,64,768]{2,1,0:T(8,128)(2,1)S(1)}, u32[]{:S(2)}, u32[]{:S(2)}) async-start(bf16[8,64,768]{2,1,0:T(8,128)(2,1)} %copy.430), calls=%async_computation.4 | async-start | bytes 1572864 | tf_op jit(solution)/shard_map/all_to_all | solution.py:434
  169.4 537.2 %reduce-scatter.20.cloned.1.call-start = ((), (), s32[]{:S(2)}) async-start(), calls=%async_computation.29 | async-start | bytes 1622016 | tf_op jit(solution)/shard_map/reduce_scatter | solution.py:514
  185.5 139.1 %copy-start.28 = (bf16[2,64,768]{2,1,0:T(8,128)(2,1)}, bf16[2,64,768]{2,1,0:T(8,128)(2,1)S(1)}, u32[]{:S(2)}) copy-start(bf16[2,64,768]{2,1,0:T(8,128)(2,1)S(1)} %copy.412) | copy-start | bytes 589828
  186.2 105.4 %copy-start.19 = (bf16[2,64,768]{2,1,0:T(8,128)(2,1)}, bf16[2,64,768]{2,1,0:T(8,128)(2,1)S(1)}, u32[]{:S(2)}) copy-start(bf16[2,64,768]{2,1,0:T(8,128)(2,1)S(1)} %copy.432) | copy-start | bytes 589828
  194.4 30.6 %copy-start.2 = (bf16[512,768]{0,1:T(8,128)(2,1)}, bf16[512,768]{0,1:T(8,128)(2,1)S(1)}, u32[]{:S(2)}) copy-start(bf16[512,768]{0,1:T(8,128)(2,1)S(1)} %copy.420) | copy-start | bytes 2359300
  538.3 208.5 %reduce-scatter.8.cloned.1.call-start = ((), (), s32[]{:S(2)}) async-start(), calls=%async_computation.23 | async-start | bytes 2433024 | tf_op jit(solution)/shard_map/reduce_scatter | solution.py:514
  550.5 301.1 %reduce-scatter.10.cloned.1.call-start = ((), (), s32[]{:S(2)}) async-start(), calls=%async_computation.24 | async-start | bytes 2433024 | tf_op jit(solution)/shard_map/reduce_scatter | solution.py:514
  563.6 391.8 %reduce-scatter.12.cloned.1.call-start = ((), (), s32[]{:S(2)}) async-start(), calls=%async_computation.25 | async-start | bytes 2433024 | tf_op jit(solution)/shard_map/reduce_scatter | solution.py:514
  570.8 489.4 %reduce-scatter.14.cloned.1.call-start = ((), (), s32[]{:S(2)}) async-start(), calls=%async_computation.26 | async-start | bytes 2433024 | tf_op jit(solution)/shard_map/reduce_scatter | solution.py:514
  574.2 626.7 %reduce-scatter.16.cloned.1.call-start = ((), (), s32[]{:S(2)}) async-start(), calls=%async_computation.27 | async-start | bytes 9732096 | tf_op jit(solution)/shard_map/reduce_scatter | solution.py:514
  582.7 760.3 %reduce-scatter.18.cloned.1.call-start = ((), (), s32[]{:S(2)}) async-start(), calls=%async_computation.28 | async-start | bytes 9732096 | tf_op jit(solution)/shard_map/reduce_scatter | solution.py:514
  594.3 17.7 %all-to-all-start.5 = ((bf16[8,64,768]{2,1,0:T(8,128)(2,1)}), bf16[8,64,768]{2,1,0:T(8,128)(2,1)}, u32[]{:S(2)}, u32[]{:S(2)}) async-start(bf16[8,64,768]{2,1,0:T(8,128)(2,1)} %copy.443), calls=%async_computation.5 | async-start | bytes 1572864 | tf_op jit(solution)/shard_map/all_to_all | solution.py:501
  611.9 16.4 %all-to-all-start.2 = ((bf16[8,64,768]{2,1,0:T(8,128)(2,1)}), bf16[8,64,768]{2,1,0:T(8,128)(2,1)S(1)}, u32[]{:S(2)}, u32[]{:S(2)}) async-start(bf16[8,64,768]{2,1,0:T(8,128)(2,1)} %copy.425), calls=%async_computation.2 | async-start | bytes 1572864 | tf_op jit(solution)/shard_map/all_to_all | solution.py:501
  628.4 55.7 %all-to-all-start.9 = ((bf16[8,64,768]{2,1,0:T(8,128)(2,1)}), bf16[8,64,768]{2,1,0:T(8,128)(2,1)S(1)}, u32[]{:S(2)}, u32[]{:S(2)}) async-start(bf16[8,64,768]{2,1,0:T(8,128)(2,1)} %copy.471), calls=%async_computation.9 | async-start | bytes 1572864 | tf_op jit(solution)/shard_map/all_to_all | solution.py:502
  632.7 55.0 %copy-start.166 = (s32[2]{0:T(128)S(1)}, s32[2]{0:T(128)}, u32[]{:S(2)}) copy-start(s32[2]{0:T(128)} %copy-done.165) | copy-start | bytes 28
  634.1 55.5 %copy-start.160 = (s32[2]{0:T(128)S(1)}, s32[2]{0:T(128)}, u32[]{:S(2)}) copy-start(s32[2]{0:T(128)} %copy-done.159) | copy-start | bytes 28
  684.0 20.4 %all-to-all-start.7 = ((bf16[8,64,768]{2,1,0:T(8,128)(2,1)}), bf16[8,64,768]{2,1,0:T(8,128)(2,1)S(1)}, u32[]{:S(2)}, u32[]{:S(2)}) async-start(bf16[8,64,768]{2,1,0:T(8,128)(2,1)} %copy.457), calls=%async_computation.7 | async-start | bytes 1572864 | tf_op jit(solution)/shard_map/all_to_all | solution.py:502
  (189 other events, 737.8 us)
Sparse Core Ops, SparseCore 0:
  10.9 57.6 all-gather.6
  71.5 57.9 all-gather.10
  132.4 56.6 all-gather.8
  191.9 53.8 all-gather.12
  248.5 62.5 all-gather.14
  313.9 62.4 all-gather.16
  538.4 98.0 reduce-scatter.19
  642.3 104.4 reduce-scatter.7
  753.5 98.0 reduce-scatter.9
  857.3 98.0 reduce-scatter.11
  962.1 98.0 reduce-scatter.13
  1066.6 134.3 reduce-scatter.15
  1208.4 134.5 reduce-scatter.17
where the time goes:
time: 1370 us; the launch traced here: 1350 us
  waiting for transfers between devices  733 us (54%)
  local copies, waits for them, and re-layouts  253 us (18%)
  blocking collectives  137 us (10%)
  matrix products  136 us (10%)
  starting transfers between devices  47.3 us (3%)
  other arithmetic  27 us (2%)
  between operations  16.6 us (1%)
    reduce_scatter x7, waiting for transfers between devices, on_device(): lax.psum_scatter(totals, ('dp', 'fsdp'), scatter_dimension=0, tiled=True)  636 us
    unnamed x2, blocking collectives  85.4 us
    unnamed x444, local copies, waits for them, and re-layouts  83.8 us
    all_gather x1, blocking collectives, on_device(): lax.all_gather(shards[6], ('dp', 'fsdp'), axis=0, tiled=True)  44.8 us
    all_gather x1, waiting for transfers between devices, on_device(): lax.all_gather(shards[5], ('dp', 'fsdp'), axis=0, tiled=True)  39.4 us
    dot_general x16, matrix products, left_sum(): lax.dot_general(left, right, (((0,), (0,)), ((), ())), preferred_element_...  29.5 us
  transfers between devices with their start and end apart: 22, of which 12 were waited for; matrix products, arithmetic and copies ran while one was open for 18% of the time, Pallas kernels for 0%

commit v1 on v0

v1 whole, which is shorter than its diff:
```python
import jax
import jax.numpy as jnp
from jax import lax
from jax.experimental import pallas as pl
from jax.experimental.pallas import tpu as pltpu
from jax.sharding import PartitionSpec as P

HEADS = 12
HEAD = 64
POS = 256
MICRO = 2
PAGE = 64
VECS = 16

EPS = 1e-07
ROOT_HALF = 0.7071067811865476
ROOT_TWO_PI = 2.5066282746310002
SCALE = (3.0 * HEAD) ** (-0.5)
ALL = ("dp", "fsdp")
F32 = jnp.float32
BF16 = jnp.bfloat16

B_QUERY, B_KEY, B_VALUE, B_OUTPUT, B_OUTER = 0, 1, 2, 3, 4
ATTN_GAIN, ATTN_SHIFT, FFN_GAIN, FFN_SHIFT, REL_GAIN, REL_SHIFT, B_INNER = 5, 6, 7, 8, 9, 10, 11


def dot(left, right):
    return jnp.dot(left, right, preferred_element_type=F32)


def dot_tn(left, right):
    return lax.dot_general(left, right, (((0,), (0,)), ((), ())), preferred_element_type=F32)


def dot_nt(left, right):
    return lax.dot_general(left, right, (((1,), (1,)), ((), ())), preferred_element_type=F32)


def column_sum(value):
    return jnp.sum(value.astype(F32), axis=0, keepdims=True)


def normalize(value):
    centered = value - jnp.mean(value, axis=-1, keepdims=True)
    inv_dev = lax.rsqrt(jnp.mean(centered * centered, axis=-1, keepdims=True) + EPS)
    return centered * inv_dev, inv_dev


def normalize_back(grad_out, unit, inv_dev, gain):
    scaled = grad_out * gain
    mixed = scaled - jnp.mean(scaled, axis=-1, keepdims=True)
    mixed = mixed - unit * jnp.mean(scaled * unit, axis=-1, keepdims=True)
    return mixed * inv_dev


def one_hot_rows(bucket_ref, count):
    rows = bucket_ref.shape[0]
    return (bucket_ref[...] == lax.broadcasted_iota(jnp.int32, (rows, count), 1)).astype(BF16)


def skewed(dist):
    rows = dist.shape[0]
    return pltpu.roll(dist, rows + 1, 1, stride=1, stride_axis=0)[:, :rows]


def attention_forward(
    x_ref, wq_ref, wk_ref, wv_ref, rel_ref, vec_ref, bucket_ref, seg_col_ref, seg_row_ref,
    q_ref, k_ref, v_ref, pq_ref, pk_ref, rel_low_ref, prob_ref, context_ref,
):
    rows = seg_row_ref.shape[1]
    bins = seg_row_ref.shape[0]
    pair = 2 * HEAD
    x = x_ref[...]
    vec = vec_ref[...].astype(F32)
    row = lambda at: vec[at : at + 1]
    q_ref[...] = (dot(x, wq_ref[...]) + row(B_QUERY)).astype(BF16)
    k_ref[...] = (dot(x, wk_ref[...]) + row(B_KEY)).astype(BF16)
    v_ref[...] = (dot(x, wv_ref[...]) + row(B_VALUE)).astype(BF16)
    unit, _ = normalize(dot(one_hot_rows(bucket_ref, rel_ref.shape[0]), rel_ref[...]))
    rel_low = (unit * row(REL_GAIN) + row(REL_SHIFT)).astype(BF16)
    rel_low_ref[...] = rel_low
    pq_ref[...] = (dot(rel_low, wq_ref[...]) + row(B_QUERY)).astype(BF16)
    pk_ref[...] = (dot(rel_low, wk_ref[...]) + row(B_KEY)).astype(BF16)
    first = lax.broadcasted_iota(jnp.int32, (rows, pair), 1) < HEAD
    firsts = lax.broadcasted_iota(jnp.int32, (bins * rows, pair), 1) < HEAD
    same = [
        seg_col_ref[b * rows : (b + 1) * rows, :] == seg_row_ref[b : b + 1, :] for b in range(bins)
    ]

    def body(step, carry):
        lanes = pl.ds(pl.multiple_of(step * pair, pair), pair)
        q, k, v = q_ref[:, lanes], k_ref[:, lanes], v_ref[:, lanes]
        pq, pk = pq_ref[:, lanes], pk_ref[:, lanes]
        parts = [[None] * 2 for _ in range(bins)]
        for h in range(2):
            own = firsts if h == 0 else jnp.logical_not(firsts)
            qh = jnp.where(own, q, jnp.zeros_like(q))
            kh = jnp.where(own, k, jnp.zeros_like(k))
            to_pos = dot_nt(qh, pk)
            to_cont = dot_nt(kh, pq)
            for b in range(bins):
                at = slice(b * rows, (b + 1) * rows)
                scores = dot_nt(qh[at], k[at]) + skewed(to_pos[at]) + skewed(to_cont[at]).T
                masked = jnp.where(same[b], SCALE * scores, -1e30)
                power = jnp.exp(masked - jnp.max(masked, axis=-1, keepdims=True))
                prob = power / jnp.sum(power, axis=-1, keepdims=True)
                prob_ref[(step * 2 + h) * bins + b] = prob
                parts[b][h] = dot(prob.astype(BF16), v[at])
        for b in range(bins):
            context_ref[b * rows : (b + 1) * rows, lanes] = jnp.where(
                first, parts[b][0], parts[b][1]
            ).astype(BF16)
        return carry

    lax.fori_loop(0, HEADS // 2, body, 0)


def ffn_forward(
    context_ref, x_ref, wo_ref, wi_ref, wout_ref, vec_ref, cot_ref,
    result_ref, unit_one_ref, inv_one_ref, hidden_low_ref, slope_ref, grad_res_ref, grad_outer_ref,
    grad_wout_ref, sums_ref,
):
    chunks = wi_ref.shape[0]
    vec = vec_ref[...].astype(F32)
    row = lambda at: vec[at : at + 1]
    attended = dot(context_ref[...], wo_ref[...]) + row(B_OUTPUT)
    unit, inv = normalize(attended + x_ref[...].astype(F32))
    unit_one_ref[...] = unit
    inv_one_ref[...] = inv
    hidden = unit * row(ATTN_GAIN) + row(ATTN_SHIFT)
    hidden_low = hidden.astype(BF16)
    hidden_low_ref[...] = hidden_low
    total = hidden + row(B_OUTER)
    active = []
    for c in range(chunks):
        inner = dot(hidden_low, wi_ref[c]) + row(B_INNER + c)
        phi = 0.5 * (1.0 + lax.erf(inner * ROOT_HALF))
        slope_ref[c] = phi + inner * jnp.exp(-0.5 * inner * inner) / ROOT_TWO_PI
        active.append((inner * phi).astype(BF16))
        total = total + dot(active[c], wout_ref[c])
    unit, inv = normalize(total)
    result_ref[...] = (unit * row(FFN_GAIN) + row(FFN_SHIFT)).astype(BF16)
    cot = cot_ref[...].astype(F32)
    grad_res = normalize_back(cot, unit, inv, row(FFN_GAIN))
    grad_res_ref[...] = grad_res
    grad_outer = grad_res.astype(BF16)
    grad_outer_ref[...] = grad_outer
    sums_ref[...] = jnp.concatenate(
        [column_sum(grad_outer), column_sum(cot * unit), column_sum(cot)]
        + [jnp.zeros_like(cot[:1])] * 5,
        axis=0,
    )
    for c in range(chunks):
        grad_wout_ref[c] = dot_tn(active[c], grad_outer).astype(BF16)


def ffn_backward(
    grad_outer_ref, grad_res_ref, slope_ref, hidden_low_ref, unit_one_ref, inv_one_ref, context_ref,
    wo_ref, wi_ref, wout_ref, vec_ref,
    grad_wi_ref, grad_wo_ref, grad_one_ref, grad_context_ref, sums_ref,
):
    chunks = wi_ref.shape[0]
    vec = vec_ref[...].astype(F32)
    row = lambda at: vec[at : at + 1]
    grad_outer = grad_outer_ref[...]
    hidden_low = hidden_low_ref[...]
    grad_hidden = grad_res_ref[...]
    bias = []
    for c in range(chunks):
        grad_inner = (dot_nt(grad_outer, wout_ref[c]) * slope_ref[c]).astype(BF16)
        grad_wi_ref[c] = dot_tn(hidden_low, grad_inner).astype(BF16)
        bias.append(column_sum(grad_inner))
        grad_hidden = grad_hidden + dot_nt(grad_inner, wi_ref[c])
    unit = unit_one_ref[...]
    grad_one = normalize_back(grad_hidden, unit, inv_one_ref[...], row(ATTN_GAIN))
    grad_one_ref[...] = grad_one
    grad_att = grad_one.astype(BF16)
    sums_ref[...] = jnp.concatenate(
        bias
        + [column_sum(grad_att), column_sum(grad_hidden * unit), column_sum(grad_hidden)]
        + [jnp.zeros_like(bias[0])] * (5 - chunks),
        axis=0,
    )
    grad_context_ref[...] = dot_nt(grad_att, wo_ref[...]).astype(BF16)
    grad_wo_ref[...] = dot_tn(context_ref[...], grad_att).astype(BF16)


def attention_backward(
    grad_context_ref, grad_one_ref, x_ref, q_ref, k_ref, v_ref, pq_ref, pk_ref, rel_low_ref, prob_ref,
    wq_ref, wk_ref, wv_ref, rel_ref, vec_ref, bucket_ref,
    grad_wq_ref, grad_wk_ref, grad_wv_ref, grad_rel_ref, grad_in_ref, sums_ref,
    dq_ref, dk_ref, dv_ref, dpq_ref, dpk_ref, qf_ref, kf_ref,
):
    bins = prob_ref.shape[0] // HEADS
    rows = prob_ref.shape[1]
    pair = 2 * HEAD
    first = lax.broadcasted_iota(jnp.int32, (rows, pair), 1) < HEAD
    firsts = lax.broadcasted_iota(jnp.int32, (2 * rows, pair), 1) < HEAD
    flip = (
        lax.broadcasted_iota(jnp.int32, (rows, rows), 0)
        + lax.broadcasted_iota(jnp.int32, (rows, rows), 1)
        == rows - 1
    ).astype(BF16)
    for b in range(bins):
        at = slice(b * rows, (b + 1) * rows)
        qf_ref[at, :] = dot(flip, q_ref[at, :]).astype(BF16)
        kf_ref[at, :] = dot(flip, k_ref[at, :]).astype(BF16)

    def unskewed(square):
        wide = jnp.concatenate([square, jnp.zeros_like(square)], axis=1)
        return pltpu.roll(wide, 0, 1, stride=1, stride_axis=0).astype(BF16)

    def unflip(value):
        high = value.astype(BF16)
        return dot(flip, high) + dot(flip, (value - high.astype(F32)).astype(BF16))

    def body(step, carry):
        lanes = pl.ds(pl.multiple_of(step * pair, pair), pair)
        q, k, v = q_ref[:, lanes], k_ref[:, lanes], v_ref[:, lanes]
        pq, pk = pq_ref[:, lanes], pk_ref[:, lanes]
        qf, kf, dc = qf_ref[:, lanes], kf_ref[:, lanes], grad_context_ref[:, lanes]
        dpq, dpk = [], []
        grads = [[None] * 2 for _ in range(bins)]
        for h in range(2):
            own = first if h == 0 else jnp.logical_not(first)
            to_pos, to_cont = [], []
            for b in range(bins):
                at = slice(b * rows, (b + 1) * rows)
                prob = prob_ref[(step * 2 + h) * bins + b]
                dch = jnp.where(own, dc[at], jnp.zeros_like(dc[at]))
                grad_prob = dot_nt(dch, v[at])
                dv = dot_tn(prob.astype(BF16), dc[at])
                dots = jnp.sum(prob * grad_prob, axis=-1, keepdims=True)
                score = (prob * (grad_prob - dots)).astype(BF16)
                by_pos = unskewed(dot(flip, score))
                by_cont = unskewed(dot_nt(flip, score))
                to_pos.append(by_pos)
                to_cont.append(by_cont)
                dq = dot(score, k[at]) + unflip(dot(by_pos, pk))
                dk = dot_tn(score, q[at]) + unflip(dot(by_cont, pq))
                grads[b][h] = (dq, dk, dv)
            dpk.append(dot_tn(jnp.concatenate(to_pos, axis=0), qf))
            dpq.append(dot_tn(jnp.concatenate(to_cont, axis=0), kf))
        for b in range(bins):
            at = slice(b * rows, (b + 1) * rows)
            (dq0, dk0, dv0), (dq1, dk1, dv1) = grads[b]
            dq_ref[at, lanes] = (SCALE * jnp.where(first, dq0, dq1)).astype(BF16)
            dk_ref[at, lanes] = (SCALE * jnp.where(first, dk0, dk1)).astype(BF16)
            dv_ref[at, lanes] = jnp.where(first, dv0, dv1).astype(BF16)
        dpq_ref[:, lanes] = (SCALE * jnp.where(firsts, dpq[0], dpq[1])).astype(BF16)
        dpk_ref[:, lanes] = (SCALE * jnp.where(firsts, dpk[0], dpk[1])).astype(BF16)
        return carry

    lax.fori_loop(0, HEADS // 2, body, 0)
    vec = vec_ref[...].astype(F32)
    x, rel_low = x_ref[...], rel_low_ref[...]
    dq, dk, dv, dpq, dpk = dq_ref[...], dk_ref[...], dv_ref[...], dpq_ref[...], dpk_ref[...]
    grad_wq_ref[...] = (dot_tn(x, dq) + dot_tn(rel_low, dpq)).astype(BF16)
    grad_wk_ref[...] = (dot_tn(x, dk) + dot_tn(rel_low, dpk)).astype(BF16)
    grad_wv_ref[...] = dot_tn(x, dv).astype(BF16)
    wq, wk = wq_ref[...], wk_ref[...]
    grad_in_ref[...] = (
        grad_one_ref[...] + dot_nt(dq, wq) + dot_nt(dk, wk) + dot_nt(dv, wv_ref[...])
    ).astype(BF16)
    choose = one_hot_rows(bucket_ref, rel_ref.shape[0])
    unit, inv = normalize(dot(choose, rel_ref[...]))
    grad_low = dot_nt(dpq, wq) + dot_nt(dpk, wk)
    grad_rel = normalize_back(grad_low, unit, inv, vec[REL_GAIN : REL_GAIN + 1])
    high = grad_rel.astype(BF16)
    low = (grad_rel - high.astype(F32)).astype(BF16)
    grad_rel_ref[...] = (dot_tn(choose, high) + dot_tn(choose, low)).astype(BF16)
    sums_ref[...] = jnp.concatenate(
        [
            column_sum(dq) + column_sum(dpq),
            column_sum(dk) + column_sum(dpk),
            column_sum(dv),
            column_sum(grad_low * unit),
            column_sum(grad_low),
        ]
        + [jnp.zeros_like(grad_low[:1])] * 3,
        axis=0,
    )


def kernel_call(body, name, outs, scratch=(), flops=0, moved=0):
    space = pl.BlockSpec(memory_space=pltpu.VMEM)

    def call(*args):
        return pl.pallas_call(
            body,
            name=name,
            out_shape=[jax.ShapeDtypeStruct(shape, kind) for shape, kind in outs],
            in_specs=[space] * len(args),
            out_specs=[space] * len(outs),
            scratch_shapes=list(scratch),
            cost_estimate=pl.CostEstimate(flops=flops, bytes_accessed=moved, transcendentals=0),
        )(*args)

    return call


def on_device(
    tokens, cotangent, routes, lengths, buckets,
    w_query, w_key, w_value, w_output, w_inner, w_outer, relative,
    b_query, b_key, b_value, b_output, b_inner, b_outer,
    attn_gain, attn_shift, ffn_gain, ffn_shift, rel_gain, rel_shift,
):
    groups = lax.axis_size("fsdp")
    count = lax.axis_size("dp") * groups
    seat = lax.axis_index("fsdp")
    me = lax.axis_index("dp") * groups + seat
    both, width = tokens.shape
    rows = both // MICRO
    pages = rows // PAGE
    unit = width // count
    wide = w_inner.shape[1] // width
    dist = 2 * rows

    singles = jnp.stack(
        [b_query, b_key, b_value, b_output, b_outer, attn_gain, attn_shift, ffn_gain, ffn_shift,
         rel_gain, rel_shift]
    )
    zero = jnp.zeros((), jnp.int32)
    placed = lax.dynamic_update_slice(
        jnp.zeros((singles.shape[0], width), BF16), singles, (zero, me * unit)
    )
    inner_placed = lax.dynamic_update_slice(
        jnp.zeros((wide * width,), BF16), b_inner, (me * b_inner.shape[0],)
    ).reshape(wide, width)
    vec_part = jnp.concatenate(
        [placed, inner_placed, jnp.zeros((VECS - singles.shape[0] - wide, width), BF16)], axis=0
    )
    inner_part = w_inner.reshape(unit, wide, width).transpose(1, 0, 2).reshape(unit * wide, width)
    pack = jnp.concatenate(
        [w_query, w_key, w_value, relative, vec_part, w_output, inner_part, w_outer], axis=0
    )
    full = lax.all_gather(pack, ALL, axis=0, tiled=False)
    cuts = [0]
    for part in (w_query, w_key, w_value, relative, vec_part, w_output, inner_part, w_outer):
        cuts.append(cuts[-1] + part.shape[0])
    piece = lambda at: full[:, cuts[at] : cuts[at + 1]]
    wq, wk, wv, rel = [piece(at).reshape(-1, width) for at in range(4)]
    vec = jnp.sum(piece(4).astype(F32), axis=0)
    wo = piece(5).reshape(-1, width)
    wi = piece(6).reshape(count, wide, unit, width).transpose(1, 0, 2, 3).reshape(wide, width, width)
    wout = piece(7).reshape(wide, width, width)

    table = lax.all_gather(routes, "fsdp", axis=0, tiled=False)
    target = routes // pages
    pick = (target[:, None, :] == jnp.arange(groups, dtype=jnp.int32)[None, :, None]).astype(BF16)
    slots = seat * pages + jnp.arange(pages, dtype=jnp.int32)
    place = jnp.any(
        table.transpose(1, 0, 2)[:, None, :, :] == slots[None, :, None, None], axis=3
    ).astype(BF16)
    own = jnp.stack([tokens, cotangent]).reshape(2, MICRO, pages, PAGE * width)
    send = jnp.einsum("mgk,amkr->gamr", pick, own, preferred_element_type=F32).astype(BF16)
    got = lax.all_to_all(send, "fsdp", split_axis=0, concat_axis=0, tiled=True)
    binned = jnp.einsum("mps,samr->ampr", place, got, preferred_element_type=F32).astype(BF16)
    binned = binned.reshape(2, both, width)
    x, cot = binned[0], binned[1]

    bounds = jnp.cumsum(lengths, axis=1)[:, :-1]
    segment = jnp.sum(
        (jnp.arange(rows, dtype=jnp.int32)[None, :, None] >= bounds[:, None, :]).astype(jnp.int32),
        axis=2,
    )
    bucket_col = jnp.concatenate([jnp.flip(buckets), jnp.full((1,), -1, jnp.int32)])[:, None]

    low = (both, width)
    q, k, v, pq, pk, rel_low, prob, context = kernel_call(
        attention_forward, "attention_forward",
        [(low, BF16)] * 3 + [((dist, width), BF16)] * 3
        + [((MICRO * HEADS, rows, rows), F32), (low, BF16)],
    )(x, wq, wk, wv, rel, vec, bucket_col, segment.reshape(both, 1), segment)
    result, unit_one, inv_one, hidden_low, slope, grad_res, grad_outer, grad_wout, sums_a = kernel_call(
        ffn_forward, "ffn_forward",
        [(low, BF16), (low, F32), ((both, 1), F32), (low, BF16), ((wide,) + low, F32), (low, F32),
         (low, BF16), ((wide, width, width), BF16), ((8, width), F32)],
    )(context, x, wo, wi, wout, vec, cot)
    grad_wi, grad_wo, grad_one, grad_context, sums_b = kernel_call(
        ffn_backward, "ffn_backward",
        [((wide, width, width), BF16), ((width, width), BF16), (low, F32), (low, BF16),
         ((8, width), F32)],
    )(grad_outer, grad_res, slope, hidden_low, unit_one, inv_one, context, wo, wi, wout, vec)
    grad_wq, grad_wk, grad_wv, grad_rel, grad_in, sums_c = kernel_call(
        attention_backward, "attention_backward",
        [((width, width), BF16)] * 3 + [(rel.shape, BF16), (low, BF16), ((8, width), F32)],
        [pltpu.VMEM(low, BF16)] * 3 + [pltpu.VMEM((dist, width), BF16)] * 2
        + [pltpu.VMEM(low, BF16)] * 2,
    )(grad_context, grad_one, x, q, k, v, pq, pk, rel_low, prob, wq, wk, wv, rel, vec, bucket_col)

    sums = jnp.concatenate([sums_a, sums_b, sums_c], axis=0).astype(BF16)
    sent = jnp.concatenate(
        [
            grad_wq.reshape(count, -1, width),
            grad_wk.reshape(count, -1, width),
            grad_wv.reshape(count, -1, width),
            grad_rel.reshape(count, -1, width),
            jnp.broadcast_to(sums[None], (count,) + sums.shape),
            grad_wo.reshape(count, -1, width),
            grad_wi.reshape(wide, count, unit, width).transpose(1, 0, 2, 3).reshape(count, -1, width),
            grad_wout.reshape(count, -1, width),
        ],
        axis=1,
    )
    mine = lax.psum_scatter(sent, ALL, scatter_dimension=0, tiled=False).astype(F32)
    ends = [0]
    for size in (unit, unit, unit, relative.shape[0], sums.shape[0], unit, unit * wide, unit * wide):
        ends.append(ends[-1] + size)
    take = lambda at: mine[ends[at] : ends[at + 1]]
    g_inner = take(6).reshape(wide, unit, width).transpose(1, 0, 2).reshape(unit, wide * width)
    vectors = lax.dynamic_slice(take(4), (zero, me * unit), (sums.shape[0], unit))
    v_inner = lax.dynamic_slice(
        take(4)[8 : 8 + wide].reshape(-1), (me * b_inner.shape[0],), b_inner.shape
    )

    done = jnp.stack([result, grad_in]).reshape(2, MICRO, pages, PAGE * width)
    back = jnp.einsum("mps,ampr->samr", place, done, preferred_element_type=F32).astype(BF16)
    home = lax.all_to_all(back, "fsdp", split_axis=0, concat_axis=0, tiled=True)
    home = jnp.einsum("mgk,gamr->amkr", pick, home, preferred_element_type=F32).astype(BF16)
    home = home.reshape(2, both, width)
    return (
        home[0], home[1], take(0), take(1), take(2), take(5), g_inner, take(7), take(3),
        vectors[16], vectors[17], vectors[18], vectors[8 + wide], v_inner, vectors[0],
        vectors[9 + wide], vectors[10 + wide], vectors[1], vectors[2], vectors[19], vectors[20],
    )


def solution(mesh):
    flat = P(ALL)
    rows = P(ALL, None)
    in_specs = (rows,) * 4 + (P(),) + (rows,) * 7 + (flat,) * 12
    out_specs = (rows,) * 9 + (flat,) * 12
    return jax.shard_map(
        on_device, mesh=mesh, in_specs=in_specs, out_specs=out_specs, check_vma=False
    )
```

time: 1370 us -> 463 us (0.34); the launches traced: 1350 us -> 457 us
  waiting for transfers between devices: 733 us -> 232 us
  local copies, waits for them, and re-layouts: 253 us -> 74.7 us
  matrix products: 136 us -> 6.34 us
  blocking collectives: 137 us -> 49.4 us
  Pallas kernels: 0 us -> 65.9 us
  starting transfers between devices: 47.3 us -> 9.42 us
  other arithmetic: 27 us -> 4.17 us
    reduce_scatter x7 -> x1, waiting for transfers between devices: 636 us -> 133 us  [on_device(): lax.psum_scatter(sent, ALL, scatter_dimension=0, tiled=False).astype(F32)]
    dot_general x90 -> x4, matrix products: 136 us -> 6.34 us  [the longest x1 2.12 us: on_device(): jnp.einsum('mgk,gamr->amkr', pick, home, preferred_element_type=F32)]
    unnamed x2 -> x0, blocking collectives: 85.4 us -> none
    unnamed x444 -> x37, local copies, waits for them, and re-layouts: 83.8 us -> 13.6 us
    pallas_call x0 -> x4, Pallas kernels: none -> 65.9 us  [call(): pl.pallas_call(body, name=name, out_shape=[jax.ShapeDtypeStruct(shape, ki...]
    reshape x17 -> x6, local copies, waits for them, and re-layouts: 62.1 us -> 4.92 us  [the longest x1 2.44 us: on_device(): piece(6).reshape(count, wide, unit, width).transpose(1, 0, 2, 3)]
    all_to_all x9 -> x2, starting transfers between devices: 34.5 us -> 9.34 us  [the longest x1 5.38 us: on_device(): got = lax.all_to_all(send, 'fsdp', split_axis=0, concat_axis=0, tiled=True)]
    dot_general x6 -> x0, local copies, waits for them, and re-layouts: 22.1 us -> none  [the longest x2 10.3 us: score_all(): jnp.einsum('jhd,bhd->hjb', keyed, pos_query, preferred_element_type=jnp.f...]
  transfers between devices with their start and end apart: 22 -> 4, of which waited for: 12 -> 3; matrix products, arithmetic and copies ran while one was open for 18% -> 6% of each run, Pallas kernels for 0% -> 0%
where the time goes in v1:
time: 463 us; the launch traced here: 457 us
  waiting for transfers between devices  232 us (50%)
  local copies, waits for them, and re-layouts  74.7 us (16%)
  Pallas kernels  65.9 us (14%)
  blocking collectives  49.4 us (11%)
  between operations  14.8 us (3%)
  starting transfers between devices  9.42 us (2%)
  matrix products  6.34 us (1%)
    reduce_scatter x1, waiting for transfers between devices, on_device(): lax.psum_scatter(sent, ALL, scatter_dimension=0, tiled=False).astype(F32)  133 us
    pallas_call x4, Pallas kernels, call(): pl.pallas_call(body, name=name, out_shape=[jax.ShapeDtypeStruct(shape, ki...  65.9 us
    all_gather x1, waiting for transfers between devices, on_device(): full = lax.all_gather(pack, ALL, axis=0, tiled=False)  60.9 us
    all_gather x1, blocking collectives, on_device(): table = lax.all_gather(routes, 'fsdp', axis=0, tiled=False)  49.4 us
    all_to_all x1, waiting for transfers between devices, on_device(): home = lax.all_to_all(back, 'fsdp', split_axis=0, concat_axis=0, tiled=True)  37.8 us
    unnamed x37, local copies, waits for them, and re-layouts  13.6 us
    slice x3, local copies, waits for them, and re-layouts, on_device(): piece = lambda at: full[:, cuts[at]:cuts[at + 1]]  13.3 us
    concatenate x1, local copies, waits for them, and re-layouts, on_device(): jnp.concatenate([w_query, w_key, w_value, relative, vec_part, w_output, i...  11 us
  transfers between devices with their start and end apart: 4, of which 3 were waited for; matrix products, arithmetic and copies ran while one was open for 6% of the time, Pallas kernels for 0%

profile of v1, /device:TPU:0, one launch (start us, length us, event | category | flops | bytes accessed | tf_op | source)
XLA Modules:
  0.0 456.9 jit_solution(6470005466995177229)
XLA Ops:
  9.1 1.5 stack.68
  10.8 11.0 %concatenate.19 = bf16[320,768]{1,0:T(8,128)(2,1)} concatenate(bf16[24,768]{1,0:T(8,128)(2,1)} %param.29, bf16[24,768]{1,0:T(8,128)(2,1)} %param.30, bf16[24,768]{1,0:T(8,128)(2,1)} %param.31, bf16[16,768]{1,0:T(8,128)(2,1)} %param.35, bf16[11,768]{1,0:T(8,128)(2,1)S(1)} %dynamic_update_slice.6, bf16[4,768]{1,0:T(4,128)(2,1)S(1)} %reshape.195, ...), dimensions={0} | concatenate | bytes 983040 | tf_op jit(solution)/shard_map/concatenate | solution.py:334
  24.0 1.1 fusion
  25.1 4.9 %copy.86 = bf16[8,2,2,49152]{3,1,2,0:T(2,128)(2,1)} copy(bf16[8,2,2,49152]{3,0,1,2:T(8,128)(2,1)S(1)} %fusion) | data formatting | bytes 6291456 | tf_op jit(solution)/shard_map/convert_element_type | solution.py:356
  30.0 5.4 %all-to-all-start = ((bf16[8,2,2,49152]{3,1,2,0:T(2,128)(2,1)}), bf16[8,2,2,49152]{3,1,2,0:T(2,128)(2,1)S(1)}, u32[]{:S(2)}, u32[]{:S(2)}) async-start(bf16[8,2,2,49152]{3,1,2,0:T(2,128)(2,1)} %copy.86), calls=%async_computation | async-start | bytes 6291456 | tf_op jit(solution)/shard_map/all_to_all | solution.py:357
  35.5 49.4 %all-gather.2 = s32[8,2,2]{2,1,0:T(2,128)S(1)} all-gather(s32[1,2,2]{2,1,0:T(2,128)S(1)} %bitcast.154), channel_id=2, replica_groups=mesh['dp'=4,'fsdp'=8] {'fsdp'}, dimensions={0}, use_global_device_ids=true | all-gather | bytes 144 | tf_op jit(solution)/shard_map/all_gather | solution.py:348
  87.1 2.1 fusion.2
  91.8 60.9 %all-gather.5.cloned.1.call-done = bf16[10240,768]{1,0:T(8,128)(2,1)} async-done(((bf16[320,768]{1,0:T(8,128)(2,1)}), bf16[10240,768]{1,0:T(8,128)(2,1)}) %all-gather.5.cloned.1.call-update) | async-done | bytes 15728656 | tf_op jit(solution)/shard_map/all_gather | solution.py:337
  152.7 4.6 fusion.33
  157.3 1.9 convert_reduce_fusion.vec_ref
  159.2 2.1 slice.180
  161.3 6.6 %fusion.32 = (bf16[32,96,768]{2,1,0:T(8,128)(2,1)}, bf16[32,96,768]{2,1,0:T(8,128)(2,1)S(1)}) fusion(bf16[32,320,768]{2,1,0:T(8,128)(2,1)} %bitcast.125), kind=kLoop, calls=%fused_computation.73 | loop fusion | bytes 18874368 | tf_op jit(solution)/shard_map/slice | solution.py:341
  167.9 2.4 copy.92
  170.3 14.2 %attention_forward.1 = (bf16[256,768]{1,0:T(8,128)(2,1)}, bf16[256,768]{1,0:T(8,128)(2,1)}, bf16[256,768]{1,0:T(8,128)(2,1)}, bf16[256,768]{1,0:T(8,128)(2,1)}, ...) custom-call(bf16[256,768]{1,0:T(8,128)(2,1)} %squeeze.45.x_ref, ...), custom_call_target="tpu_custom_call" | custom-call | tf_op jit(solution)/shard_map/attention_forward/pallas_call | solution.py:289
  184.5 12.4 %ffn_forward.1 = (bf16[256,768]{1,0:T(8,128)(2,1)}, f32[256,768]{1,0:T(8,128)}, f32[256,1]{1,0:T(8,128)}, bf16[256,768]{1,0:T(8,128)(2,1)}, f32[4,256,768]{2,1,0...) custom-call(bf16[256,768]{1,0:T(8,128)(2,1)} %get-tuple-element.49.c, ...), custom_call_target="tpu_custom_call" | custom-call | tf_op jit(solution)/shard_map/ffn_forward/pallas_call | solution.py:289
  196.9 12.4 %ffn_backward.1 = (bf16[4,768,768]{2,1,0:T(8,128)(2,1)}, bf16[768,768]{1,0:T(8,128)(2,1)}, f32[256,768]{1,0:T(8,128)}, bf16[256,768]{1,0:T(8,128)(2,1)}, f32[8,768]{1,0:T(8,128)}) custom-call(bf16[256,768]{1,0:T(8,128)(2,1)} %get-tuple-element.51.grad_outer_ref, f32[256,768]{1,0:T(8,128)} %get-tuple-element.52.grad_res_ref, ...), custom_call_target="tpu_custom_call" | custom-call | tf_op jit(solution)/shard_map/ffn_backward/pallas_call | solution.py:289
  209.4 26.9 %attention_backward.1 = (bf16[768,768]{1,0:T(8,128)(2,1)}, bf16[768,768]{1,0:T(8,128)(2,1)}, bf16[768,768]{1,0:T(8,128)(2,1)}, bf16[512,768]{1,0:T(8,128)(2,1)},...) custom-call(bf16[256,768]{1,0:T(8,128)(2,1)} %get-tuple-element.57.grad_context_ref, ...), custom_call_target="tpu_custom_call" | custom-call | tf_op jit(solution)/shard_map/attention_backward/pallas_call | solution.py:289
  237.0 2.4 constant_dynamic-update-slice_fusion.6
  239.4 3.0 copy.98
  242.5 1.1 constant_dynamic-update-slice_fusion.5
  244.2 1.1 constant_dynamic-update-slice_fusion.4
  246.3 1.2 broadcast_dynamic-update-slice_fusion
  247.4 1.1 constant_dynamic-update-slice_fusion.2
  248.6 2.7 constant_dynamic-update-slice_fusion.1
  251.3 1.2 slice-done
  252.6 2.5 constant_dynamic-update-slice_fusion
  257.3 4.9 %copy.96 = bf16[8,2,2,49152]{3,1,2,0:T(2,128)(2,1)} copy(bf16[8,2,2,49152]{3,0,1,2:T(8,128)(2,1)S(1)} %fusion.1) | data formatting | bytes 6291456 | tf_op jit(solution)/shard_map/convert_element_type | solution.py:418
  262.2 4.0 all-to-all-start.1
  266.1 37.8 %all-to-all-done.1 = bf16[8,2,2,49152]{3,1,2,0:T(2,128)(2,1)S(1)} async-done(((bf16[8,2,2,49152]{3,1,2,0:T(2,128)(2,1)}), bf16[8,2,2,49152]{3,1,2,0:T(2,128)(2,1)S(1)}, u32[]{:S(2)}, u32[]{:S(2)}) %all-to-all-start.1) | async-done | bytes 3145760 | tf_op jit(solution)/shard_map/all_to_all | solution.py:419
  303.9 2.1 fusion.3
  308.6 133.4 %reduce-scatter.2.cloned.1.call-done = bf16[1,328,768]{2,1,0:T(8,128)(2,1)} async-done(((bf16[32,328,768]{2,1,0:T(8,128)(2,1)}), bf16[1,328,768]{2,1,0:T(8,128)(2,1)}) %reduce-scatter.2.cloned.1.call-update) | async-done | bytes 503824 | tf_op jit(solution)/shard_map/reduce_scatter | solution.py:406
  442.0 1.1 convert_element_type.51
  (77 shorter events, 22.7 us)
Async XLA Ops:
  7.2 16.8 %copy-start.9 = (s32[2,2]{1,0:T(2,128)S(1)}, s32[2,2]{1,0:T(2,128)}, u32[]{:S(2)}) copy-start(s32[2,2]{1,0:T(2,128)} %param.26) | copy-start | bytes 52
  7.2 145.5 %all-gather.5.cloned.1.call-start = ((), (), s32[]{:S(2)}) async-start(), calls=%async_computation.4 | async-start | bytes 16220160 | tf_op jit(solution)/shard_map/all_gather | solution.py:337
  30.0 54.9 %copy-start.10 = (s32[255]{0:T(256)S(1)}, s32[255]{0:T(256)}, u32[]{:S(2)}) copy-start(s32[255]{0:T(256)} %param.28) | copy-start | bytes 3064
  30.0 55.9 %copy-start.11 = (s32[2,3]{1,0:T(2,128)S(1)}, s32[2,3]{1,0:T(2,128)}, u32[]{:S(2)}) copy-start(s32[2,3]{1,0:T(2,128)} %param.27) | copy-start | bytes 76
  30.0 57.1 %all-to-all-start = ((bf16[8,2,2,49152]{3,1,2,0:T(2,128)(2,1)}), bf16[8,2,2,49152]{3,1,2,0:T(2,128)(2,1)S(1)}, u32[]{:S(2)}, u32[]{:S(2)}) async-start(bf16[8,2,2,49152]{3,1,2,0:T(2,128)(2,1)} %copy.86), calls=%async_computation | async-start | bytes 6291456 | tf_op jit(solution)/shard_map/all_to_all | solution.py:357
  35.4 406.6 %reduce-scatter.2.cloned.1.call-start = ((), (), s32[]{:S(2)}) async-start(), calls=%async_computation.3 | async-start | bytes 16625664 | tf_op jit(solution)/shard_map/reduce_scatter | solution.py:406
  86.2 4.5 copy-start.8
  209.4 27.7 %copy-start.7 = (f32[8,768]{1,0:T(8,128)S(1)}, f32[8,768]{1,0:T(8,128)}, u32[]{:S(2)}) copy-start(f32[8,768]{1,0:T(8,128)} %get-tuple-element.72) | copy-start | bytes 73732
  209.4 27.7 %copy-start.6 = (f32[8,768]{1,0:T(8,128)S(1)}, f32[8,768]{1,0:T(8,128)}, u32[]{:S(2)}) copy-start(f32[8,768]{1,0:T(8,128)} %get-tuple-element.71) | copy-start | bytes 73732
  239.4 3.1 copy-start.2
  242.5 1.7 copy-start.1
  242.5 2.8 copy-start.3
  243.7 3.8 copy-start
  248.6 3.9 slice-start
  248.6 4.0 slice-start.1
  255.0 1.0 copy-start.5
  255.0 1.1 copy-start.4
  262.2 41.8 %all-to-all-start.1 = ((bf16[8,2,2,49152]{3,1,2,0:T(2,128)(2,1)}), bf16[8,2,2,49152]{3,1,2,0:T(2,128)(2,1)S(1)}, u32[]{:S(2)}, u32[]{:S(2)}) async-start(bf16[8,2,2,49152]{3,1,2,0:T(2,128)(2,1)} %copy.96), calls=%async_computation.1 | async-start | bytes 6291456 | tf_op jit(solution)/shard_map/all_to_all | solution.py:419
Sparse Core Ops, SparseCore 0:
  21.9 130.7 all-gather.4
  255.2 186.8 reduce-scatter.1
